TPU v7x, 256 devices: a whole 4x4x8 slice. The times are simulated.
256 devices in a mesh: section: 32 (over z_lo, y, core), tensor: 8 (over z_hi, x).
Axes of the slice: x: 4, y: 4, z: 8 (z_hi: 2, z_lo: 4; z = z_hi * 4 + z_lo), core: 2. Of those that a mesh axis runs over, the one named last changes fastest.
Arguments:
- queries: bfloat16 [8192, 4096], P('section', 'tensor'), may hold values from -180 to 180
- memory: bfloat16 [512, 4096], P('section', 'tensor'), may hold values from -6 to 6
- key_weight: bfloat16 [65536, 4096], P('section', 'tensor'), may hold values from -0.09375 to 0.09375
- value_weight: bfloat16 [65536, 4096], P('section', 'tensor'), may hold values from -0.09375 to 0.09375
- grad_context: bfloat16 [8192, 4096], P('section', 'tensor'), may hold values from -6 to 6
- memory_lengths: int32 [4], replicated, may hold values from 64 to 128, as said below
Outputs:
- context: bfloat16 [8192, 4096], P('section', 'tensor')
- grad_queries: bfloat16 [8192, 4096], P('section', 'tensor')
- grad_memory: float32 [512, 4096], P('section', 'tensor')
Inputs may be any that keep to these rules, and one draw needn't show every extreme that they name: `memory_lengths`: one reaction in every draw has all 128 encoder tokens.
All inputs are finite; a program needn't handle non-finite values.
Results may differ from a plain program's by a relative error of at most 0.0171.
The roundings to bfloat16 on the way count: a program that leaves them out, or rounds other values in their place, can miss the bound.
Values may be sent and summed in bfloat16 or wider, within the bound.
No kernel may reach another device: no remote copies, remote signals or barrier semaphores. Data moves between devices by JAX's collectives and lax.ppermute only.
A program may use at most 64 MiB of HBM per device.

v0:
```python
import jax
import jax.numpy as jnp
from jax import lax
from jax.sharding import PartitionSpec as P

HDIM = 64


def partner(block, axis, distance):
    count = lax.axis_size(axis)
    route = []
    for low in range(count):
        high = low | 1 << distance
        if high != low and high < count:
            route += [(low, high), (high, low)]
    return lax.ppermute(block, axis, route)


def times_transposed(left, weight_rows):
    return lax.dot_general(
        left, weight_rows, (((1,), (1,)), ((), ())), preferred_element_type=jnp.float32
    )


def body(queries, memory, key_weight, value_weight, grad_context, memory_lengths):
    scale = HDIM ** (-0.5)
    parity = lax.axis_index("section") % 2
    react = memory_lengths.shape[0]
    half_react = react // 2
    head_cols = queries.shape[1]
    local_heads = head_cols // HDIM
    half_width = key_weight.shape[0]
    full_width = 2 * half_width
    half_start = parity * half_width
    full_rows = lax.all_gather(memory, "tensor", axis=1, tiled=True)
    own_cols = lax.dynamic_slice_in_dim(
        lax.all_gather(full_rows, "section", axis=0, tiled=True), half_start, half_width, 1
    )
    key_part = jnp.dot(own_cols, key_weight, preferred_element_type=jnp.float32)
    value_part = jnp.dot(own_cols, value_weight, preferred_element_type=jnp.float32)
    joined = jnp.concatenate([key_part, value_part], axis=1)
    key_all = joined[:, :head_cols]
    value_all = joined[:, head_cols:]
    half_rows = key_all.shape[0] // 2
    is_first = parity == 0
    own_key = jnp.where(is_first, key_all[:half_rows], key_all[half_rows:])
    other_key = jnp.where(is_first, key_all[half_rows:], key_all[:half_rows])
    own_value = jnp.where(is_first, value_all[:half_rows], value_all[half_rows:])
    other_value = jnp.where(is_first, value_all[half_rows:], value_all[:half_rows])
    recv_key, recv_value = partner((other_key, other_value), "section", 0)
    keys = (own_key + recv_key).astype(jnp.bfloat16)
    values = (own_value + recv_value).astype(jnp.bfloat16)
    lengths = lax.dynamic_slice_in_dim(memory_lengths, parity * half_react, half_react, 0)
    enc_len = keys.shape[0] // half_react
    dec_len = queries.shape[0] // half_react
    query_h = queries.reshape(half_react, dec_len, local_heads, HDIM)
    key_h = keys.reshape(half_react, enc_len, local_heads, HDIM)
    value_h = values.reshape(half_react, enc_len, local_heads, HDIM)
    cot_h = grad_context.reshape(half_react, dec_len, local_heads, HDIM)
    scores = (
        jnp.einsum("rqhd,rkhd->rhqk", query_h, key_h, preferred_element_type=jnp.float32) * scale
    )
    valid = jnp.arange(enc_len, dtype=jnp.int32)[None, :] < lengths[:, None]
    scores = jnp.where(valid[:, None, None, :], scores, jnp.float32(-1e30))
    top = jnp.max(scores, axis=-1, keepdims=True)
    expo = jnp.exp(scores - top)
    probs = expo / jnp.sum(expo, axis=-1, keepdims=True)
    probs_b = probs.astype(jnp.bfloat16)
    context = jnp.einsum(
        "rhqk,rkhd->rqhd", probs_b, value_h, preferred_element_type=jnp.float32
    ).astype(jnp.bfloat16)
    grad_p = jnp.einsum("rqhd,rkhd->rhqk", cot_h, value_h, preferred_element_type=jnp.float32)
    delta = jnp.sum(probs * grad_p, axis=-1, keepdims=True)
    grad_s = (probs * (grad_p - delta) * scale).astype(jnp.bfloat16)
    grad_q = jnp.einsum(
        "rhqk,rkhd->rqhd", grad_s, key_h, preferred_element_type=jnp.float32
    ).astype(jnp.bfloat16)
    key_grad = jnp.einsum(
        "rhqk,rqhd->rkhd", grad_s, query_h, preferred_element_type=jnp.float32
    ).astype(jnp.bfloat16)
    value_grad = jnp.einsum(
        "rhqk,rqhd->rkhd", probs_b, cot_h, preferred_element_type=jnp.float32
    ).astype(jnp.bfloat16)
    key_grad = key_grad.reshape(half_react * enc_len, head_cols)
    value_grad = value_grad.reshape(half_react * enc_len, head_cols)
    partner_key, partner_value = partner((key_grad, value_grad), "section", 0)
    layer_key_grad = jnp.where(
        is_first,
        jnp.concatenate([key_grad, partner_key], axis=0),
        jnp.concatenate([partner_key, key_grad], axis=0),
    )
    layer_value_grad = jnp.where(
        is_first,
        jnp.concatenate([value_grad, partner_value], axis=0),
        jnp.concatenate([partner_value, value_grad], axis=0),
    )
    block = times_transposed(layer_key_grad, key_weight) + times_transposed(
        layer_value_grad, value_weight
    )
    blank_rows = jnp.zeros((block.shape[0], full_width), jnp.float32)
    layer_total = lax.psum_scatter(
        lax.dynamic_update_slice_in_dim(blank_rows, block, half_start, 1),
        "section",
        scatter_dimension=0,
        tiled=True,
    )
    grad_memory = lax.psum_scatter(layer_total, "tensor", scatter_dimension=1, tiled=True)
    return (
        context.reshape(half_react * dec_len, head_cols),
        grad_q.reshape(half_react * dec_len, head_cols),
        grad_memory,
    )


def solution(mesh):
    placed = (
        P("section", "tensor"),
        P("section", "tensor"),
        P("section", "tensor"),
        P("section", "tensor"),
        P("section", "tensor"),
        P(),
    )
    return jax.shard_map(
        body,
        mesh=mesh,
        in_specs=placed,
        out_specs=(P("section", "tensor"), P("section", "tensor"), P("section", "tensor")),
        check_vma=False,
    )
```

profile of v0, /device:TPU:8, one launch (start us, length us, event | category | flops | bytes accessed | tf_op | source)
XLA Modules:
  0.0 410.7 jit_solution(8636467715947990893)
XLA Ops:
  7.2 48.3 %all_gather.6 = bf16[16,4096]{1,0:T(8,128)(2,1)} all-gather(bf16[16,512]{1,0:T(8,128)(2,1)} %param.7), channel_id=1, replica_groups=mesh['section'=32,'tensor'=8] {'tensor'}, dimensions={1}, use_global_device_ids=true | all-gather | bytes 147456 | tf_op jit(solution)/shard_map/all_gather | solution.py:35
  55.6 63.2 %all-gather.2.cloned.1.call-done = bf16[512,4096]{1,0:T(8,128)(2,1)} async-done(((bf16[16,4096]{1,0:T(8,128)(2,1)}), bf16[512,4096]{1,0:T(8,128)(2,1)}) %all-gather.2.cloned.1.call-update) | async-done | bytes 4194320 | tf_op jit(solution)/shard_map/all_gather | solution.py:37
  118.8 3.0 fusion.2
  123.0 1.2 fusion.4
  126.5 2.0 copy.26
  128.6 2.1 reshape.63
  130.6 1.3 copy.33
  132.2 2.2 add_convert_fusion
  134.3 2.1 reshape.61
  136.4 2.0 copy.25
  138.4 1.9 add_convert_fusion.1
  140.3 1.3 reshape.60
  142.7 2.6 fusion.50
  146.7 1.4 convolution_bitcast_fusion
  148.1 3.0 fusion.16
  151.1 1.2 copy.39
  152.9 3.1 fusion.27
  156.0 4.2 %broadcast_in_dim.23 = f32[512,4096]{1,0:T(8,128)} broadcast(f32[]{:T(128)} %constant.34.clone.1), dimensions={} | broadcast | bytes 8388612 | tf_op jit(solution)/shard_map/broadcast_in_dim | solution.py:100
  160.3 3.4 add_dynamic-update-slice_fusion
  163.7 150.6 %reduce-scatter.3.cloned.1.call-done = f32[16,4096]{1,0:T(8,128)} async-done(((f32[512,4096]{1,0:T(8,128)}), f32[16,4096]{1,0:T(8,128)}) %reduce-scatter.3.cloned.1.call-update) | async-done | bytes 262160 | tf_op jit(solution)/shard_map/reduce_scatter | solution.py:101
  314.3 2.9 fusion.15
  317.2 1.2 copy.50
  319.5 1.8 fusion.14
  322.7 81.5 %reduce-scatter.5.cloned.1.call-done = f32[16,512]{1,0:T(8,128)} async-done(((f32[16,4096]{1,0:T(8,128)}), f32[16,512]{1,0:T(8,128)}) %reduce-scatter.5.cloned.1.call-update) | async-done | bytes 32784 | tf_op jit(solution)/shard_map/reduce_scatter | solution.py:107
  (47 shorter events, 9.2 us)
Async XLA Ops:
  7.2 111.6 %copy-start = (bf16[2048,512]{1,0:T(8,128)(2,1)S(1)}, bf16[2048,512]{1,0:T(8,128)(2,1)}, u32[]{:S(2)}) copy-start(bf16[2048,512]{1,0:T(8,128)(2,1)} %param.8) | copy-start | bytes 6291460
  7.2 111.6 %all-gather.2.cloned.1.call-start = ((), (), s32[]{:S(2)}) async-start(), calls=%async_computation.2 | async-start | bytes 4325376 | tf_op jit(solution)/shard_map/all_gather | solution.py:37
  55.6 258.7 %reduce-scatter.3.cloned.1.call-start = ((), (), s32[]{:S(2)}) async-start(), calls=%async_computation.3 | async-start | bytes 8650752 | tf_op jit(solution)/shard_map/reduce_scatter | solution.py:101
  118.8 4.2 %copy-start.2 = (bf16[2048,512]{1,0:T(8,128)(2,1)S(1)}, bf16[2048,512]{1,0:T(8,128)(2,1)}, u32[]{:S(2)}) copy-start(bf16[2048,512]{1,0:T(8,128)(2,1)} %param.9) | copy-start | bytes 6291460
  118.8 4.2 %copy-start.8 = (bf16[512,4096]{1,0:T(8,128)(2,1)S(1)}, bf16[512,4096]{1,0:T(8,128)(2,1)}, u32[]{:S(2)}) copy-start(bf16[512,4096]{1,0:T(8,128)(2,1)} %all-gather.2.cloned.1.call-done) | copy-start | bytes 12582916
  121.8 2.5 copy-start.1
  122.8 2.7 copy-start.4
  122.8 9.4 %collective-permute-start.1 = (f32[256,512]{1,0:T(8,128)}, f32[256,512]{1,0:T(8,128)}, u32[]{:S(2)}, u32[]{:S(2)}) collective-permute-start(f32[256,512]{1,0:T(8,128)} %slice_select_fusion), channel_id=1, source_target_pairs={{0,8},{8,0},{16,24},{24,16},{32,40},{40,32},{48,56},{56,48},{64,72... | collective-permute-start | bytes 1572872 | tf_op jit(solution)/shard_map/ppermute | solution.py:16
  124.3 7.7 %copy-start.9 = (s32[4]{0:T(128)S(1)}, s32[4]{0:T(128)}, u32[]{:S(2)}) copy-start(s32[4]{0:T(128)} %param.11) | copy-start | bytes 52
  125.2 13.3 %collective-permute-start = (f32[256,512]{1,0:T(8,128)}, f32[256,512]{1,0:T(8,128)}, u32[]{:S(2)}, u32[]{:S(2)}) collective-permute-start(f32[256,512]{1,0:T(8,128)} %slice_select_fusion.1), channel_id=1, source_target_pairs={{0,8},{8,0},{16,24},{24,16},{32,40},{40,32},{48,56},{56,48},{64,72... | collective-permute-start | bytes 1572872 | tf_op jit(solution)/shard_map/ppermute | solution.py:16
  132.0 13.3 %copy-start.3 = (bf16[2,128,8,64]{1,3,2,0:T(8,128)(2,1)}, bf16[2,128,8,64]{1,3,2,0:T(8,128)(2,1)S(1)}, u32[]{:S(2)}) copy-start(bf16[2,128,8,64]{1,3,2,0:T(8,128)(2,1)S(1)} %copy.33) | copy-start | bytes 786436
  140.3 5.0 %copy-start.5 = (bf16[2,128,8,64]{1,3,2,0:T(8,128)(2,1)S(1)}, bf16[2,128,8,64]{1,3,2,0:T(8,128)(2,1)}, u32[]{:S(2)}) copy-start(bf16[2,128,8,64]{1,3,2,0:T(8,128)(2,1)} %copy.26) | copy-start | bytes 786436
  140.3 5.0 %copy-start.6 = (bf16[2,128,8,64]{1,3,2,0:T(8,128)(2,1)S(1)}, bf16[2,128,8,64]{1,3,2,0:T(8,128)(2,1)}, u32[]{:S(2)}) copy-start(bf16[2,128,8,64]{1,3,2,0:T(8,128)(2,1)} %copy.25) | copy-start | bytes 786436
  146.4 6.5 %collective-permute-start.3 = (bf16[256,512]{0,1:T(8,128)(2,1)S(1)}, bf16[256,512]{0,1:T(8,128)(2,1)}, u32[]{:S(2)}, u32[]{:S(2)}) collective-permute-start(bf16[256,512]{0,1:T(8,128)(2,1)S(1)} %bitcast.62), channel_id=1, source_target_pairs={{0,8},{8,0},{16,24},{24,16},{32,40},{40,32},{48,56},{56,48},{64,72... | collective-permute-start | bytes 786440 | tf_op jit(solution)/shard_map/ppermute | solution.py:16
  152.4 3.6 collective-permute-start.2
  163.6 150.7 %copy-start.7 = (bf16[2,128,8,64]{1,3,2,0:T(8,128)(2,1)S(1)}, bf16[2,128,8,64]{1,3,2,0:T(8,128)(2,1)}, u32[]{:S(2)}) copy-start(bf16[2,128,8,64]{1,3,2,0:T(8,128)(2,1)} %copy.25) | copy-start | bytes 786436
  163.7 240.5 %reduce-scatter.5.cloned.1.call-start = ((), (), s32[]{:S(2)}) async-start(), calls=%async_computation.4 | async-start | bytes 294912 | tf_op jit(solution)/shard_map/reduce_scatter | solution.py:107
Sparse Core Ops, SparseCore 0:
  55.7 63.0 all-gather.1
  163.8 150.4 reduce-scatter.2
  318.7 85.4 reduce-scatter.4
where the time goes:
time: 411 us
  waiting for transfers between devices  295 us (72%)
  blocking collectives  48.3 us (12%)
  matrix products  23.2 us (6%)
  local copies, waits for them, and re-layouts  22.5 us (5%)
  between operations  13.9 us (3%)
  other arithmetic  5.97 us (1%)
    reduce_scatter x1, waiting for transfers between devices, body(): lax.psum_scatter(lax.dynamic_update_slice_in_dim(blank_rows, block, half_...  151 us
    reduce_scatter x1, waiting for transfers between devices, body(): lax.psum_scatter(layer_total, 'tensor', scatter_dimension=1, tiled=True)  81.5 us
    all_gather x1, waiting for transfers between devices, body(): lax.all_gather(full_rows, 'section', axis=0, tiled=True)  63.2 us
    all_gather x1, blocking collectives, body(): full_rows = lax.all_gather(memory, 'tensor', axis=1, tiled=True)  48.3 us
  transfers between devices with their start and end apart: 7, of which 3 were waited for; matrix products, arithmetic and copies ran while one was open for 8% of the time, Pallas kernels for 0%

commit v1 on v0

--- a/solution.py
+++ b/solution.py
@@ -32,7 +32,9 @@
     half_width = key_weight.shape[0]
     full_width = 2 * half_width
     half_start = parity * half_width
-    full_rows = lax.all_gather(memory, "tensor", axis=1, tiled=True)
+    full_rows = jnp.concatenate(
+        lax.all_to_all(jnp.stack([memory] * lax.axis_size("tensor")), "tensor", 0, 0), axis=1
+    )
     own_cols = lax.dynamic_slice_in_dim(
         lax.all_gather(full_rows, "section", axis=0, tiled=True), half_start, half_width, 1
     )

time: 411 us -> 381 us (0.927)
  blocking collectives: 48.3 us -> 21.2 us
    all_gather x1 -> x0, blocking collectives: 48.3 us -> none  [body(): full_rows = lax.all_gather(memory, 'tensor', axis=1, tiled=True)]
    all_to_all x0 -> x1, blocking collectives: none -> 21.2 us  [body(): lax.all_to_all(jnp.stack([memory] * lax.axis_size('tensor')), 'tensor', 0...]
    all_gather x1, waiting for transfers between devices: 63.2 us -> 58.4 us  [body(): lax.all_gather(full_rows, 'section', axis=0, tiled=True)]
where the time goes in v1:
time: 381 us; the launch traced here: 380 us
  waiting for transfers between devices  291 us (76%)
  local copies, waits for them, and re-layouts  24 us (6%)
  matrix products  23.2 us (6%)
  blocking collectives  21.2 us (6%)
  between operations  13.9 us (4%)
  other arithmetic  5.97 us (2%)
    reduce_scatter x1, waiting for transfers between devices, body(): lax.psum_scatter(lax.dynamic_update_slice_in_dim(blank_rows, block, half_...  151 us
    reduce_scatter x1, waiting for transfers between devices, body(): lax.psum_scatter(layer_total, 'tensor', scatter_dimension=1, tiled=True)  81.1 us
    all_gather x1, waiting for transfers between devices, body(): lax.all_gather(full_rows, 'section', axis=0, tiled=True)  58.4 us
    all_to_all x1, blocking collectives, body(): lax.all_to_all(jnp.stack([memory] * lax.axis_size('tensor')), 'tensor', 0...  21.2 us
  transfers between devices with their start and end apart: 7, of which 3 were waited for; matrix products, arithmetic and copies ran while one was open for 8% of the time, Pallas kernels for 0%

profile of v1, /device:TPU:8, one launch (start us, length us, event | category | flops | bytes accessed | tf_op | source)
XLA Modules:
  0.0 380.3 jit_solution(13283717167567610874)
XLA Ops:
  8.1 21.2 %all_to_all.5 = bf16[8,16,512]{2,1,0:T(8,128)(2,1)S(1)} all-to-all(bf16[8,16,512]{2,1,0:T(8,128)(2,1)S(1)} %stack.2), channel_id=1, replica_groups=mesh['section'=32,'tensor'=8] {'tensor'}, dimensions={0} | all-to-all | bytes 262144 | tf_op jit(solution)/shard_map/all_to_all | solution.py:36
  30.1 58.4 %all-gather.2.cloned.1.call-done = bf16[512,4096]{1,0:T(8,128)(2,1)} async-done(((bf16[16,4096]{1,0:T(8,128)(2,1)}), bf16[512,4096]{1,0:T(8,128)(2,1)}) %all-gather.2.cloned.1.call-update) | async-done | bytes 4194320 | tf_op jit(solution)/shard_map/all_gather | solution.py:39
  88.5 3.0 fusion.2
  92.7 1.2 fusion.4
  96.2 2.0 copy.50
  98.2 2.1 reshape.73
  100.3 1.3 copy.57
  101.8 2.2 add_convert_fusion
  104.0 2.1 reshape.71
  106.1 2.0 copy.49
  108.1 1.9 add_convert_fusion.1
  110.0 1.3 reshape.70
  112.3 2.6 fusion.50
  116.4 1.4 convolution_bitcast_fusion
  117.8 3.0 fusion.16
  120.8 1.2 copy.63
  122.6 3.1 fusion.27
  125.7 4.2 %broadcast_in_dim.23 = f32[512,4096]{1,0:T(8,128)} broadcast(f32[]{:T(128)} %constant.34.clone.1), dimensions={} | broadcast | bytes 8388612 | tf_op jit(solution)/shard_map/broadcast_in_dim | solution.py:102
  130.0 3.4 add_dynamic-update-slice_fusion
  133.4 151.0 %reduce-scatter.3.cloned.1.call-done = f32[16,4096]{1,0:T(8,128)} async-done(((f32[512,4096]{1,0:T(8,128)}), f32[16,4096]{1,0:T(8,128)}) %reduce-scatter.3.cloned.1.call-update) | async-done | bytes 262160 | tf_op jit(solution)/shard_map/reduce_scatter | solution.py:103
  284.4 2.9 fusion.15
  287.3 1.2 copy.74
  289.6 1.8 fusion.14
  292.7 81.1 %reduce-scatter.5.cloned.1.call-done = f32[16,512]{1,0:T(8,128)} async-done(((f32[16,4096]{1,0:T(8,128)}), f32[16,512]{1,0:T(8,128)}) %reduce-scatter.5.cloned.1.call-update) | async-done | bytes 32784 | tf_op jit(solution)/shard_map/reduce_scatter | solution.py:109
  (49 shorter events, 10.7 us)
Async XLA Ops:
  7.2 81.3 %copy-start = (bf16[2048,512]{1,0:T(8,128)(2,1)S(1)}, bf16[2048,512]{1,0:T(8,128)(2,1)}, u32[]{:S(2)}) copy-start(bf16[2048,512]{1,0:T(8,128)(2,1)} %param.8) | copy-start | bytes 6291460
  7.2 81.3 %all-gather.2.cloned.1.call-start = ((), (), s32[]{:S(2)}) async-start(), calls=%async_computation.3 | async-start | bytes 4325376 | tf_op jit(solution)/shard_map/all_gather | solution.py:39
  30.0 254.4 %reduce-scatter.3.cloned.1.call-start = ((), (), s32[]{:S(2)}) async-start(), calls=%async_computation.4 | async-start | bytes 8650752 | tf_op jit(solution)/shard_map/reduce_scatter | solution.py:103
  88.5 4.2 %copy-start.2 = (bf16[2048,512]{1,0:T(8,128)(2,1)S(1)}, bf16[2048,512]{1,0:T(8,128)(2,1)}, u32[]{:S(2)}) copy-start(bf16[2048,512]{1,0:T(8,128)(2,1)} %param.9) | copy-start | bytes 6291460
  88.5 4.2 %copy-start.8 = (bf16[512,4096]{1,0:T(8,128)(2,1)S(1)}, bf16[512,4096]{1,0:T(8,128)(2,1)}, u32[]{:S(2)}) copy-start(bf16[512,4096]{1,0:T(8,128)(2,1)} %all-gather.2.cloned.1.call-done) | copy-start | bytes 12582916
  91.5 2.5 copy-start.1
  92.5 2.7 copy-start.4
  92.5 9.4 %collective-permute-start.1 = (f32[256,512]{1,0:T(8,128)}, f32[256,512]{1,0:T(8,128)}, u32[]{:S(2)}, u32[]{:S(2)}) collective-permute-start(f32[256,512]{1,0:T(8,128)} %slice_select_fusion), channel_id=1, source_target_pairs={{0,8},{8,0},{16,24},{24,16},{32,40},{40,32},{48,56},{56,48},{64,72... | collective-permute-start | bytes 1572872 | tf_op jit(solution)/shard_map/ppermute | solution.py:16
  94.0 7.7 %copy-start.9 = (s32[4]{0:T(128)S(1)}, s32[4]{0:T(128)}, u32[]{:S(2)}) copy-start(s32[4]{0:T(128)} %param.11) | copy-start | bytes 52
  94.9 13.3 %collective-permute-start = (f32[256,512]{1,0:T(8,128)}, f32[256,512]{1,0:T(8,128)}, u32[]{:S(2)}, u32[]{:S(2)}) collective-permute-start(f32[256,512]{1,0:T(8,128)} %slice_select_fusion.1), channel_id=1, source_target_pairs={{0,8},{8,0},{16,24},{24,16},{32,40},{40,32},{48,56},{56,48},{64,72... | collective-permute-start | bytes 1572872 | tf_op jit(solution)/shard_map/ppermute | solution.py:16
  101.7 13.3 %copy-start.3 = (bf16[2,128,8,64]{1,3,2,0:T(8,128)(2,1)}, bf16[2,128,8,64]{1,3,2,0:T(8,128)(2,1)S(1)}, u32[]{:S(2)}) copy-start(bf16[2,128,8,64]{1,3,2,0:T(8,128)(2,1)S(1)} %copy.57) | copy-start | bytes 786436
  110.0 5.0 %copy-start.5 = (bf16[2,128,8,64]{1,3,2,0:T(8,128)(2,1)S(1)}, bf16[2,128,8,64]{1,3,2,0:T(8,128)(2,1)}, u32[]{:S(2)}) copy-start(bf16[2,128,8,64]{1,3,2,0:T(8,128)(2,1)} %copy.50) | copy-start | bytes 786436
  110.0 5.0 %copy-start.6 = (bf16[2,128,8,64]{1,3,2,0:T(8,128)(2,1)S(1)}, bf16[2,128,8,64]{1,3,2,0:T(8,128)(2,1)}, u32[]{:S(2)}) copy-start(bf16[2,128,8,64]{1,3,2,0:T(8,128)(2,1)} %copy.49) | copy-start | bytes 786436
  116.1 6.5 %collective-permute-start.3 = (bf16[256,512]{0,1:T(8,128)(2,1)S(1)}, bf16[256,512]{0,1:T(8,128)(2,1)}, u32[]{:S(2)}, u32[]{:S(2)}) collective-permute-start(bf16[256,512]{0,1:T(8,128)(2,1)S(1)} %bitcast.65), channel_id=1, source_target_pairs={{0,8},{8,0},{16,24},{24,16},{32,40},{40,32},{48,56},{56,48},{64,72... | collective-permute-start | bytes 786440 | tf_op jit(solution)/shard_map/ppermute | solution.py:16
  122.1 3.6 collective-permute-start.2
  133.3 151.1 %copy-start.7 = (bf16[2,128,8,64]{1,3,2,0:T(8,128)(2,1)S(1)}, bf16[2,128,8,64]{1,3,2,0:T(8,128)(2,1)}, u32[]{:S(2)}) copy-start(bf16[2,128,8,64]{1,3,2,0:T(8,128)(2,1)} %copy.49) | copy-start | bytes 786436
  133.3 240.5 %reduce-scatter.5.cloned.1.call-start = ((), (), s32[]{:S(2)}) async-start(), calls=%async_computation.5 | async-start | bytes 294912 | tf_op jit(solution)/shard_map/reduce_scatter | solution.py:109
Sparse Core Ops, SparseCore 0:
  30.1 58.3 all-gather.1
  133.5 150.8 reduce-scatter.2
  288.8 84.9 reduce-scatter.4
